TPU v7x, 512 devices: a whole 4x8x8 slice. The times are simulated.
512 devices in a mesh: grow: 32 (over x_hi, y, core), gcol: 16 (over z, x_lo).
Axes of the slice: x: 4 (x_hi: 2, x_lo: 2; x = x_hi * 2 + x_lo), y: 8, z: 8, core: 2. Of those that a mesh axis runs over, the one named last changes fastest.
Arguments:
- coefficients: bfloat16 [20480, 49152], P('grow', 'gcol'), may hold values from -0.02734375 to 0.02734375
- tile_mask: int32 [160, 384], P('grow', 'gcol'), may hold values 0 or 1
- duals: float32 [20480], P('grow'), may hold values from -6 to 6
- costs: float32 [49152], P('gcol'), may hold values from -6 to 6
- primal: float32 [49152], P('gcol'), may hold values from 0.1 to 10
- fixed: int32 [49152], P('gcol'), may hold values 0 or 1
Outputs:
- normal_window: float32 [1024, 20480], P('gcol', 'grow')
- factor_window: float32 [1024, 20480], P('gcol', 'grow')
All inputs are finite; a program needn't handle non-finite values. No bound on the sum of `tile_mask` or of `fixed` on one device may be relied on, other than what follows from the above.
Results may differ from a plain program's by a relative error of at most 0.0023.
Values may be sent and summed in bfloat16 or wider, within the bound.
A program may use at most 64 MiB of HBM per device.

v0:
```python
import jax
import jax.numpy as jnp
from jax import lax
from jax.sharding import PartitionSpec as P

PANEL = 512
SOFTNESS = 0.25
DIAGONAL_SHIFT = 0.5


def split_normal(normal, blocks_own, panel_per, rows_dev):
    split = normal.reshape(blocks_own, 2, panel_per, rows_dev)
    own_panel = split[:, 0].reshape(blocks_own * panel_per, rows_dev)
    own_trailing = split[:, 1].reshape(blocks_own * panel_per, rows_dev)
    panel_all = lax.all_gather(own_panel, "gcol", axis=0, tiled=True)
    return (own_trailing, panel_all)


def shards(coefficients, tile_mask, duals, costs, primal, fixed):
    rows_dev, columns = coefficients.shape
    row_count = lax.axis_size("grow")
    col_count = lax.axis_size("gcol")
    panel_per = PANEL // row_count
    blocks_own = row_count // col_count
    local_win = blocks_own * 2 * panel_per
    tile_rows, tile_cols = tile_mask.shape
    side = rows_dev // tile_rows
    expanded = jnp.broadcast_to(
        tile_mask[:, None, :, None], (tile_rows, side, tile_cols, side)
    ).reshape(rows_dev, columns)
    masked = coefficients * expanded.astype(jnp.bfloat16)
    partial_products = jnp.dot(
        duals, masked, preferred_element_type=jnp.float32, precision=lax.Precision.HIGHEST
    )
    products = lax.psum(partial_products, "grow")
    reduced = costs - products
    scaling = (1 - fixed).astype(jnp.float32) * primal / jnp.sqrt(reduced * reduced + SOFTNESS)
    scaled = (masked * scaling[None, :]).astype(jnp.bfloat16)
    window_all = lax.all_gather(masked[: 2 * panel_per], "grow", axis=0, tiled=True)
    col_index = lax.axis_index("gcol")
    normal = lax.psum_scatter(
        lax.dot_general(
            window_all, scaled, (((1,), (1,)), ((), ())), preferred_element_type=jnp.float32
        ),
        "gcol",
        scatter_dimension=0,
        tiled=True,
    )
    own_trailing, panel_all = split_normal(normal, blocks_own, panel_per, rows_dev)
    corner = lax.all_gather(panel_all[:, :panel_per], "grow", axis=1, tiled=True)
    shifted = 0.5 * (corner + corner.T) + DIAGONAL_SHIFT * jnp.eye(PANEL, dtype=jnp.float32)
    lower = jnp.linalg.cholesky(shifted)
    factor_panel = jax.scipy.linalg.solve_triangular(lower, panel_all, lower=True)
    edge_all = lax.all_gather(
        factor_panel[:, panel_per : 2 * panel_per], "grow", axis=1, tiled=True
    )
    own_edge = lax.dynamic_slice_in_dim(
        edge_all, col_index * (blocks_own * panel_per), blocks_own * panel_per, 1
    )
    updated = own_trailing - jnp.dot(own_edge.T, factor_panel, precision=lax.Precision.HIGHEST)
    panel_rows = lax.dynamic_slice_in_dim(
        factor_panel, col_index * (blocks_own * panel_per), blocks_own * panel_per, 0
    )
    factor = jnp.stack(
        [
            panel_rows.reshape(blocks_own, panel_per, rows_dev),
            updated.reshape(blocks_own, panel_per, rows_dev),
        ],
        axis=1,
    )
    return (normal, factor.reshape(local_win, rows_dev))


def solution(mesh):
    placed = (P("grow", "gcol"), P("grow", "gcol"), P("grow"), P("gcol"), P("gcol"), P("gcol"))
    return jax.shard_map(
        shards,
        mesh=mesh,
        in_specs=placed,
        out_specs=(P("gcol", "grow"), P("gcol", "grow")),
        check_vma=False,
    )
```

profile of v0, /device:TPU:1, one launch (start us, length us, event | category | flops | bytes accessed | tf_op | source)
XLA Modules:
  0.0 642.4 jit_solution(5346488050266648543)
XLA Ops:
  7.2 0.8 convert_element_type.17
  8.6 0.7 copy-done.2
  9.9 1.9 copy-done
  11.8 0.7 slice.145
  12.6 3.7 fusion.38
  16.3 130.1 %psum.7 = f32[3072]{0:T(1024)S(1)} all-reduce(f32[3072]{0:T(1024)S(1)} %bitcast.77), channel_id=1, replica_groups=mesh['grow'=32,'gcol'=16] {'grow'}, use_global_device_ids=true, to_apply=%region_0.0 | all-reduce | flops 3072 | bytes 24576 | tf_op jit(solution)/shard_map/psum | solution.py:35
  146.5 9.5 %fusion = f32[1024,640]{1,0:T(8,128)} fusion(bf16[1024,3072]{1,0:T(8,128)(2,1)} %all-gather.5.cloned.1.call-done, bf16[640,3072]{1,0:T(8,128)(2,1)} %copy-done, f32[3072]{0:T(1024)S(1)} %rsqrt_multiply_fusion), kind=kOutput, calls=%fused_computation.3 | convolution fusion | flops 4032430080 | bytes 12857344 | tf_op jit(solution)/shard_map/dot_general | solution.py:42
  156.0 74.2 %reduce-scatter.2.cloned.1.call-done = f32[64,640]{1,0:T(8,128)} async-done(((f32[1024,640]{1,0:T(8,128)}), f32[64,640]{1,0:T(8,128)}) %reduce-scatter.2.cloned.1.call-update) | async-done | bytes 163856 | tf_op jit(solution)/shard_map/reduce_scatter | solution.py:41
  230.3 1.6 fusion.37
  231.9 71.6 %all-gather.7.cloned.1.call-done = f32[512,640]{1,0:T(8,128)} async-done(((f32[32,640]{1,0:T(8,128)}), f32[512,640]{1,0:T(8,128)}) %all-gather.7.cloned.1.call-update) | async-done | bytes 1310736 | tf_op jit(solution)/shard_map/all_gather | solution.py:15
  303.5 1.0 slice.147
  304.5 0.7 copy.24
  305.8 94.8 %all-gather.9.cloned.1.call-done = f32[512,512]{0,1:T(8,128)} async-done(((f32[512,16]{0,1:T(8,128)}), f32[512,512]{0,1:T(8,128)}) %all-gather.9.cloned.1.call-update) | async-done | bytes 1048592 | tf_op jit(solution)/shard_map/all_gather | solution.py:50
  400.6 1.6 copy.19
  403.1 11.7 %cholesky.103 = f32[128,128]{1,0:T(8,128)S(1)} custom-call(f32[128,128]{1,0:T(8,128)S(1)} %cholesky.263), custom_call_target="Cholesky" | custom-call | tf_op jit(solution)/shard_map/jit(cholesky)/cholesky | solution.py:52
  414.8 9.8 %custom-call.31 = f32[1,128,128]{1,2,0:T(8,128)S(1)} custom-call(f32[1,128,128]{2,1,0:T(8,128)S(1)} %get-tuple-element.31), custom_call_target="InvertDiagBlocksLowerTriangular" | custom-call | tf_op jit(solution)/shard_map/jit(cholesky)/cholesky | solution.py:52
  425.1 1.0 convolution_subtract_fusion.3
  426.1 0.9 cholesky.267
  427.1 11.7 %cholesky.215 = f32[128,128]{1,0:T(8,128)S(1)} custom-call(f32[128,128]{1,0:T(8,128)S(1)} %cholesky.267), custom_call_target="Cholesky" | custom-call | tf_op jit(solution)/shard_map/jit(cholesky)/cholesky | solution.py:52
  438.8 9.9 %custom-call.32 = f32[1,128,128]{1,2,0:T(8,128)S(1)} custom-call(f32[1,128,128]{2,1,0:T(8,128)S(1)} %get-tuple-element.28), custom_call_target="InvertDiagBlocksLowerTriangular" | custom-call | tf_op jit(solution)/shard_map/jit(cholesky)/cholesky | solution.py:52
  448.7 1.2 convolution_dynamic-update-slice_fusion
  450.3 0.6 cholesky.272
  450.9 13.2 %cholesky.236 = f32[128,128]{1,0:T(8,128)} custom-call(f32[128,128]{1,0:T(8,128)} %cholesky.272), custom_call_target="Cholesky" | custom-call | tf_op jit(solution)/shard_map/jit(cholesky)/cholesky | solution.py:52
  464.1 1.5 select_reduce_fusion.1
  465.6 0.7 compare_reduce_fusion.1
  466.3 11.3 %custom-call.33 = f32[1,128,128]{1,2,0:T(8,128)} custom-call(f32[1,128,128]{2,1,0:T(8,128)} %get-tuple-element.25), custom_call_target="InvertDiagBlocksLowerTriangular" | custom-call | tf_op jit(solution)/shard_map/jit(cholesky)/cholesky | solution.py:52
  477.6 1.0 convolution_dynamic-update-slice_fusion.1
  479.0 11.9 %cholesky.253 = f32[128,128]{1,0:T(8,128)S(1)} custom-call(f32[128,128]{1,0:T(8,128)S(1)} %convolution_subtract_fusion.6), custom_call_target="Cholesky" | custom-call | tf_op jit(solution)/shard_map/jit(cholesky)/cholesky | solution.py:52
  490.9 0.7 compare_reduce_fusion
  491.7 0.6 compare_reduce_fusion.2
  494.9 10.7 %while.1 = (s32[]{:T(128)}, f32[512,512]{1,0:T(8,128)S(1)}, s32[4,2]{0,1:T(2,128)S(1)}, f32[4,128,128]{2,1,0:T(8,128)}, s32[]{:T(128)}) while((s32[]{:T(128)}, f32[512,512]{1,0:T(8,128)S(1)}, s32[4,2]{0,1:T(2,128)S(1)}, f32[4,128,128]{2,1,0:T(8,128)}, s32[]{:T(128)}) %tuple.32), condition=%wide.while_cond, body=%wide.while_body.sunk | while | flops 2 | bytes 132705 | solution.py:53
  495.0 0.6 fusion.48
  495.6 2.0 bitcast_dynamic-update-slice_fusion.2
  497.6 0.6 fusion.48
  498.2 2.0 bitcast_dynamic-update-slice_fusion.2
  500.3 0.6 fusion.48
  500.9 2.0 bitcast_dynamic-update-slice_fusion.2
  503.0 0.6 fusion.48
  503.6 2.0 bitcast_dynamic-update-slice_fusion.2
  505.6 40.1 %custom-call.34 = f32[4,128,128]{1,2,0:T(8,128)S(1)} custom-call(f32[4,128,128]{2,1,0:T(8,128)} %get-tuple-element.9), custom_call_target="InvertDiagBlocksLowerTriangular" | custom-call | tf_op jit(solution)/shard_map/jit(_solve_triangular)/triangular_solve | solution.py:53
  546.8 1.3 fusion.26
  548.7 1.3 fusion.24
  550.0 0.9 convolution_subtract_fusion.2
  550.9 1.3 fusion.23
  552.4 0.7 copy.21
  553.2 80.1 %all-gather.11.cloned.1.call-done = f32[512,512]{0,1:T(8,128)} async-done(((f32[512,16]{0,1:T(8,128)}), f32[512,512]{0,1:T(8,128)}) %all-gather.11.cloned.1.call-update) | async-done | bytes 1048592 | tf_op jit(solution)/shard_map/all_gather | solution.py:54
  633.3 1.7 convolution_subtract_fusion.5
  635.0 0.7 copy.22
  (59 shorter events, 6.3 us)
Async XLA Ops:
  7.2 139.3 %all-gather.5.cloned.1.call-start = ((), (), s32[]{:S(2)}) async-start(), calls=%async_computation.1 | async-start | bytes 6488064 | tf_op jit(solution)/shard_map/all_gather | solution.py:39
  7.2 2.1 copy-start.2
  9.3 3.2 copy-start.9
  9.9 1.9 copy-start
  11.8 134.6 %copy-start.6 = (f32[3072]{0:T(1024)S(1)}, f32[3072]{0:T(1024)}, u32[]{:S(2)}) copy-start(f32[3072]{0:T(1024)} %param.9) | copy-start | bytes 36868
  11.8 134.6 %copy-start.7 = (f32[3072]{0:T(1024)S(1)}, f32[3072]{0:T(1024)}, u32[]{:S(2)}) copy-start(f32[3072]{0:T(1024)} %param.10) | copy-start | bytes 36868
  11.8 134.6 %copy-start.8 = (s32[3072]{0:T(1024)S(1)}, s32[3072]{0:T(1024)}, u32[]{:S(2)}) copy-start(s32[3072]{0:T(1024)} %param.11) | copy-start | bytes 36868
  12.5 217.7 %reduce-scatter.2.cloned.1.call-start = ((), (), s32[]{:S(2)}) async-start(), calls=%async_computation.2 | async-start | bytes 2785280 | tf_op jit(solution)/shard_map/reduce_scatter | solution.py:41
  156.0 147.6 %all-gather.7.cloned.1.call-start = ((), (), s32[]{:S(2)}) async-start(), calls=%async_computation.3 | async-start | bytes 1392640 | tf_op jit(solution)/shard_map/all_gather | solution.py:15
  231.9 168.7 %all-gather.9.cloned.1.call-start = ((), (), s32[]{:S(2)}) async-start(), calls=%async_computation.4 | async-start | bytes 1081344 | tf_op jit(solution)/shard_map/all_gather | solution.py:50
  305.3 328.0 %all-gather.11.cloned.1.call-start = ((), (), s32[]{:S(2)}) async-start(), calls=%async_computation.5 | async-start | bytes 1081344 | tf_op jit(solution)/shard_map/all_gather | solution.py:54
  400.6 1.7 copy-start.1
  426.1 119.6 %copy-start.3 = (f32[512,640]{1,0:T(8,128)S(1)}, f32[512,640]{1,0:T(8,128)}, u32[]{:S(2)}) copy-start(f32[512,640]{1,0:T(8,128)} %all-gather.7.cloned.1.call-done) | copy-start | bytes 3932164
  545.7 0.7 copy-start.4
  550.8 82.4 %copy-start.5 = (f32[2,1,16,640]{3,2,1,0:T(8,128)S(1)}, f32[2,1,16,640]{3,2,1,0:T(8,128)}, u32[]{:S(2)}) copy-start(f32[2,1,16,640]{3,2,1,0:T(8,128)} %get-tuple-element.21) | copy-start | bytes 245764
Sparse Core Ops, SparseCore 0:
  12.6 105.7 all-gather.4
  156.1 74.1 reduce-scatter.1
  232.9 70.5 all-gather.6
  307.3 93.2 all-gather.8
  553.3 79.9 all-gather.10
where the time goes:
time: 648 us; the launch traced here: 642 us
  waiting for transfers between devices  321 us (50%)
  blocking collectives  130 us (20%)
  other arithmetic  125 us (19%)
  matrix products  25.4 us (4%)
  local copies, waits for them, and re-layouts  23.3 us (4%)
  between operations  16.8 us (3%)
    psum x1, blocking collectives, shards(): products = lax.psum(partial_products, 'grow')  130 us
    all_gather x1, waiting for transfers between devices, shards(): lax.all_gather(panel_all[:, :panel_per], 'grow', axis=1, tiled=True)  94.8 us
    another operation x14, other arithmetic, shards(): lower = jnp.linalg.cholesky(shifted)  83.1 us
    all_gather x1, waiting for transfers between devices, shards(): lax.all_gather(factor_panel[:, panel_per:2 * panel_per], 'grow', axis=1,...  80.1 us
    reduce_scatter x1, waiting for transfers between devices, shards(): lax.psum_scatter(lax.dot_general(window_all, scaled, (((1,), (1,)), ((),...  74.2 us
    all_gather x1, waiting for transfers between devices, split_normal(): panel_all = lax.all_gather(own_panel, 'gcol', axis=0, tiled=True)  71.6 us
    another operation x4, other arithmetic, shards(): jax.scipy.linalg.solve_triangular(lower, panel_all, lower=True)  40.3 us
  transfers between devices with their start and end apart: 5, of which 4 were waited for; matrix products, arithmetic and copies ran while one was open for 1% of the time, Pallas kernels for 0%

commit v1 on v0

--- a/solution.py
+++ b/solution.py
@@ -32,7 +32,8 @@
     partial_products = jnp.dot(
         duals, masked, preferred_element_type=jnp.float32, precision=lax.Precision.HIGHEST
     )
-    products = lax.psum(partial_products, "grow")
+    terms = lax.all_gather(partial_products, "grow", axis=0, tiled=False)
+    products = terms.sum(axis=0)
     reduced = costs - products
     scaling = (1 - fixed).astype(jnp.float32) * primal / jnp.sqrt(reduced * reduced + SOFTNESS)
     scaled = (masked * scaling[None, :]).astype(jnp.bfloat16)

time: 648 us -> 614 us (0.948)
  blocking collectives: 130 us -> 44.7 us
  waiting for transfers between devices: 321 us -> 372 us
    psum x1 -> x0, blocking collectives: 130 us -> none  [shards(): products = lax.psum(partial_products, 'grow')]
    all_gather x1, waiting for transfers between devices: 0.02 us -> 57.2 us  [shards(): lax.all_gather(masked[:2 * panel_per], 'grow', axis=0, tiled=True)]
    all_gather x0 -> x1, blocking collectives: none -> 44.7 us  [shards(): terms = lax.all_gather(partial_products, 'grow', axis=0, tiled=False)]
    reduce_scatter x1, waiting for transfers between devices: 74.2 us -> 67.1 us  [shards(): lax.psum_scatter(lax.dot_general(window_all, scaled, (((1,), (1,)), ((),...]
  transfers between devices with their start and end apart: 5 -> 5, of which waited for: 4 -> 5; matrix products, arithmetic and copies ran while one was open for 1% -> 1% of each run, Pallas kernels for 0% -> 0%
where the time goes in v1:
time: 614 us; the launch traced here: 609 us
  waiting for transfers between devices  372 us (61%)
  other arithmetic  125 us (20%)
  blocking collectives  44.7 us (7%)
  matrix products  25.4 us (4%)
  local copies, waits for them, and re-layouts  23.3 us (4%)
  between operations  16.8 us (3%)
    all_gather x1, waiting for transfers between devices, shards(): lax.all_gather(panel_all[:, :panel_per], 'grow', axis=1, tiled=True)  94.8 us
    another operation x14, other arithmetic, shards(): lower = jnp.linalg.cholesky(shifted)  83.2 us
    all_gather x1, waiting for transfers between devices, shards(): lax.all_gather(factor_panel[:, panel_per:2 * panel_per], 'grow', axis=1,...  80.1 us
    all_gather x1, waiting for transfers between devices, split_normal(): panel_all = lax.all_gather(own_panel, 'gcol', axis=0, tiled=True)  72.9 us
    reduce_scatter x1, waiting for transfers between devices, shards(): lax.psum_scatter(lax.dot_general(window_all, scaled, (((1,), (1,)), ((),...  67.1 us
    all_gather x1, waiting for transfers between devices, shards(): lax.all_gather(masked[:2 * panel_per], 'grow', axis=0, tiled=True)  57.2 us
    all_gather x1, blocking collectives, shards(): terms = lax.all_gather(partial_products, 'grow', axis=0, tiled=False)  44.7 us
    another operation x4, other arithmetic, shards(): jax.scipy.linalg.solve_triangular(lower, panel_all, lower=True)  40.3 us
  transfers between devices with their start and end apart: 5, of which 5 were waited for; matrix products, arithmetic and copies ran while one was open for 1% of the time, Pallas kernels for 0%

profile of v1, /device:TPU:1, one launch (start us, length us, event | category | flops | bytes accessed | tf_op | source)
XLA Modules:
  0.0 608.5 jit_solution(6522889724906054673)
XLA Ops:
  7.2 0.8 convert_element_type.17
  8.6 0.7 copy-done.2
  9.9 1.9 copy-done
  11.8 0.7 slice.145
  12.6 3.8 fusion.38
  16.4 44.7 %all-gather = f32[98304]{0:T(1024)S(1)} all-gather(f32[3072]{0:T(1024)S(1)} %bitcast.77), channel_id=2, replica_groups=mesh['grow'=32,'gcol'=16] {'grow'}, dimensions={0}, use_global_device_ids=true | all-gather | bytes 405504 | tf_op jit(solution)/shard_map/all_gather | solution.py:35
  61.2 57.2 %all-gather.6.cloned.1.call-done = bf16[1024,3072]{1,0:T(8,128)(2,1)} async-done(((bf16[32,3072]{1,0:T(8,128)(2,1)}), bf16[1024,3072]{1,0:T(8,128)(2,1)}) %all-gather.6.cloned.1.call-update) | async-done | bytes 6291472 | tf_op jit(solution)/shard_map/all_gather | solution.py:40
  118.4 9.5 %fusion = f32[1024,640]{1,0:T(8,128)} fusion(bf16[1024,3072]{1,0:T(8,128)(2,1)} %all-gather.6.cloned.1.call-done, bf16[640,3072]{1,0:T(8,128)(2,1)} %copy-done, f32[3072]{0:T(1024)S(1)} %rsqrt_multiply_fusion), kind=kOutput, calls=%fused_computation.3 | convolution fusion | flops 4032430080 | bytes 12857344 | tf_op jit(solution)/shard_map/dot_general | solution.py:43
  128.0 67.1 %reduce-scatter.2.cloned.1.call-done = f32[64,640]{1,0:T(8,128)} async-done(((f32[1024,640]{1,0:T(8,128)}), f32[64,640]{1,0:T(8,128)}) %reduce-scatter.2.cloned.1.call-update) | async-done | bytes 163856 | tf_op jit(solution)/shard_map/reduce_scatter | solution.py:42
  195.0 1.6 fusion.37
  196.7 72.9 %all-gather.8.cloned.1.call-done = f32[512,640]{1,0:T(8,128)} async-done(((f32[32,640]{1,0:T(8,128)}), f32[512,640]{1,0:T(8,128)}) %all-gather.8.cloned.1.call-update) | async-done | bytes 1310736 | tf_op jit(solution)/shard_map/all_gather | solution.py:15
  269.6 1.0 slice.147
  270.6 0.7 copy.30
  271.9 94.8 %all-gather.10.cloned.1.call-done = f32[512,512]{0,1:T(8,128)} async-done(((f32[512,16]{0,1:T(8,128)}), f32[512,512]{0,1:T(8,128)}) %all-gather.10.cloned.1.call-update) | async-done | bytes 1048592 | tf_op jit(solution)/shard_map/all_gather | solution.py:51
  366.7 1.6 copy.25
  369.2 11.7 %cholesky.103 = f32[128,128]{1,0:T(8,128)S(1)} custom-call(f32[128,128]{1,0:T(8,128)S(1)} %cholesky.263), custom_call_target="Cholesky" | custom-call | tf_op jit(solution)/shard_map/jit(cholesky)/cholesky | solution.py:53
  381.0 9.8 %custom-call.31 = f32[1,128,128]{1,2,0:T(8,128)S(1)} custom-call(f32[1,128,128]{2,1,0:T(8,128)S(1)} %get-tuple-element.31), custom_call_target="InvertDiagBlocksLowerTriangular" | custom-call | tf_op jit(solution)/shard_map/jit(cholesky)/cholesky | solution.py:53
  391.2 1.0 convolution_subtract_fusion.3
  392.2 0.9 cholesky.267
  393.2 11.7 %cholesky.215 = f32[128,128]{1,0:T(8,128)S(1)} custom-call(f32[128,128]{1,0:T(8,128)S(1)} %cholesky.267), custom_call_target="Cholesky" | custom-call | tf_op jit(solution)/shard_map/jit(cholesky)/cholesky | solution.py:53
  404.9 10.0 %custom-call.32 = f32[1,128,128]{1,2,0:T(8,128)S(1)} custom-call(f32[1,128,128]{2,1,0:T(8,128)S(1)} %get-tuple-element.28), custom_call_target="InvertDiagBlocksLowerTriangular" | custom-call | tf_op jit(solution)/shard_map/jit(cholesky)/cholesky | solution.py:53
  414.9 1.2 convolution_dynamic-update-slice_fusion
  416.4 0.6 cholesky.272
  417.1 13.2 %cholesky.236 = f32[128,128]{1,0:T(8,128)} custom-call(f32[128,128]{1,0:T(8,128)} %cholesky.272), custom_call_target="Cholesky" | custom-call | tf_op jit(solution)/shard_map/jit(cholesky)/cholesky | solution.py:53
  430.2 1.5 select_reduce_fusion.1
  431.7 0.7 compare_reduce_fusion.1
  432.4 11.3 %custom-call.33 = f32[1,128,128]{1,2,0:T(8,128)} custom-call(f32[1,128,128]{2,1,0:T(8,128)} %get-tuple-element.25), custom_call_target="InvertDiagBlocksLowerTriangular" | custom-call | tf_op jit(solution)/shard_map/jit(cholesky)/cholesky | solution.py:53
  443.7 1.0 convolution_dynamic-update-slice_fusion.1
  445.1 11.9 %cholesky.253 = f32[128,128]{1,0:T(8,128)S(1)} custom-call(f32[128,128]{1,0:T(8,128)S(1)} %convolution_subtract_fusion.6), custom_call_target="Cholesky" | custom-call | tf_op jit(solution)/shard_map/jit(cholesky)/cholesky | solution.py:53
  457.1 0.7 compare_reduce_fusion
  457.8 0.6 compare_reduce_fusion.2
  461.0 10.7 %while.1 = (s32[]{:T(128)}, f32[512,512]{1,0:T(8,128)S(1)}, s32[4,2]{0,1:T(2,128)S(1)}, f32[4,128,128]{2,1,0:T(8,128)}, s32[]{:T(128)}) while((s32[]{:T(128)}, f32[512,512]{1,0:T(8,128)S(1)}, s32[4,2]{0,1:T(2,128)S(1)}, f32[4,128,128]{2,1,0:T(8,128)}, s32[]{:T(128)}) %tuple.32), condition=%wide.while_cond, body=%wide.while_body.sunk | while | flops 2 | bytes 132705 | solution.py:54
  461.1 0.6 fusion.48
  461.7 2.0 bitcast_dynamic-update-slice_fusion.2
  463.8 0.6 fusion.48
  464.4 2.0 bitcast_dynamic-update-slice_fusion.2
  466.4 0.6 fusion.48
  467.0 2.0 bitcast_dynamic-update-slice_fusion.2
  469.7 2.0 bitcast_dynamic-update-slice_fusion.2
  471.7 40.1 %custom-call.34 = f32[4,128,128]{1,2,0:T(8,128)S(1)} custom-call(f32[4,128,128]{2,1,0:T(8,128)} %get-tuple-element.9), custom_call_target="InvertDiagBlocksLowerTriangular" | custom-call | tf_op jit(solution)/shard_map/jit(_solve_triangular)/triangular_solve | solution.py:54
  512.9 1.3 fusion.26
  514.8 1.3 fusion.24
  516.1 0.9 convolution_subtract_fusion.2
  517.0 1.3 fusion.23
  518.6 0.7 copy.27
  519.3 80.1 %all-gather.12.cloned.1.call-done = f32[512,512]{0,1:T(8,128)} async-done(((f32[512,16]{0,1:T(8,128)}), f32[512,512]{0,1:T(8,128)}) %all-gather.12.cloned.1.call-update) | async-done | bytes 1048592 | tf_op jit(solution)/shard_map/all_gather | solution.py:55
  599.4 1.7 convolution_subtract_fusion.5
  601.1 0.7 copy.28
  (61 shorter events, 7.0 us)
Async XLA Ops:
  7.2 111.3 %all-gather.6.cloned.1.call-start = ((), (), s32[]{:S(2)}) async-start(), calls=%async_computation.1 | async-start | bytes 6488064 | tf_op jit(solution)/shard_map/all_gather | solution.py:40
  7.2 2.1 copy-start.2
  9.3 3.2 copy-start.9
  9.9 1.9 copy-start
  12.5 182.5 %reduce-scatter.2.cloned.1.call-start = ((), (), s32[]{:S(2)}) async-start(), calls=%async_computation.2 | async-start | bytes 2785280 | tf_op jit(solution)/shard_map/reduce_scatter | solution.py:42
  12.6 48.6 %copy-start.6 = (f32[3072]{0:T(1024)S(1)}, f32[3072]{0:T(1024)}, u32[]{:S(2)}) copy-start(f32[3072]{0:T(1024)} %param.9) | copy-start | bytes 36868
  12.6 48.6 %copy-start.7 = (f32[3072]{0:T(1024)S(1)}, f32[3072]{0:T(1024)}, u32[]{:S(2)}) copy-start(f32[3072]{0:T(1024)} %param.10) | copy-start | bytes 36868
  12.6 48.6 %copy-start.8 = (s32[3072]{0:T(1024)S(1)}, s32[3072]{0:T(1024)}, u32[]{:S(2)}) copy-start(s32[3072]{0:T(1024)} %param.11) | copy-start | bytes 36868
  127.9 141.7 %all-gather.8.cloned.1.call-start = ((), (), s32[]{:S(2)}) async-start(), calls=%async_computation.3 | async-start | bytes 1392640 | tf_op jit(solution)/shard_map/all_gather | solution.py:15
  196.7 170.0 %all-gather.10.cloned.1.call-start = ((), (), s32[]{:S(2)}) async-start(), calls=%async_computation.4 | async-start | bytes 1081344 | tf_op jit(solution)/shard_map/all_gather | solution.py:51
  271.4 328.0 %all-gather.12.cloned.1.call-start = ((), (), s32[]{:S(2)}) async-start(), calls=%async_computation.5 | async-start | bytes 1081344 | tf_op jit(solution)/shard_map/all_gather | solution.py:55
  366.7 1.7 copy-start.1
  392.2 119.6 %copy-start.3 = (f32[512,640]{1,0:T(8,128)S(1)}, f32[512,640]{1,0:T(8,128)}, u32[]{:S(2)}) copy-start(f32[512,640]{1,0:T(8,128)} %all-gather.8.cloned.1.call-done) | copy-start | bytes 3932164
  511.8 0.7 copy-start.4
  517.0 82.4 %copy-start.5 = (f32[2,1,16,640]{3,2,1,0:T(8,128)S(1)}, f32[2,1,16,640]{3,2,1,0:T(8,128)}, u32[]{:S(2)}) copy-start(f32[2,1,16,640]{3,2,1,0:T(8,128)} %get-tuple-element.21) | copy-start | bytes 245764
Sparse Core Ops, SparseCore 0:
  12.6 105.7 all-gather.5
  128.0 66.9 reduce-scatter.1
  197.7 71.8 all-gather.7
  273.4 93.2 all-gather.9
  519.4 79.9 all-gather.11
